TPU v7x, 32 devices: a whole 2x2x4 slice. The times are simulated.
32 devices in a mesh: rad: 8 (over z, y), ell: 4 (over x, core).
Axes of the slice: x: 2, y: 2, z: 4, core: 2. Of those that a mesh axis runs over, the one named last changes fastest.
Arguments:
- field: bfloat16 [512, 128, 512], P('rad', 'ell'), may hold values from -6 to 6
- projection: bfloat16 [512, 128, 256], P('rad', 'ell'), may hold values from -0.375 to 0.375
- ell_ids: int32 [128], P('ell'), may hold values from 0 to 255, as said below
Outputs:
- share: float32 [128, 256], P('ell', 'rad')
- crest: float32 [128, 256], P('ell', 'rad')
Inputs may be any that keep to these rules, and one draw needn't show every extreme that they name: `ell_ids`: distinct and ascending.
All inputs are finite; a program needn't handle non-finite values.
Results may differ from a plain program's by a relative error of at most 0.0003.
Values may be sent and summed in bfloat16 or wider, within the bound.
A program may use at most 64 MiB of HBM per device.

v0:
```python
import jax
import jax.numpy as jnp
from jax import lax
from jax.sharding import PartitionSpec as P


def per_device(field, projection, ell_ids):
    exchanged = lax.all_to_all(field, "rad", split_axis=2, concat_axis=0, tiled=True)
    slot_share = exchanged.shape[2]
    coef = jnp.einsum(
        "rem,ren->emn",
        exchanged,
        lax.all_gather(projection, "rad", axis=0, tiled=True),
        preferred_element_type=jnp.float32,
    )
    slots = lax.axis_index("rad") * slot_share + jnp.arange(slot_share, dtype=jnp.int32)
    valid = (slots[None, :] < 2 * ell_ids[:, None] + 1).astype(jnp.float32)
    energy_part = jnp.sum(valid[:, :, None] * coef * coef, axis=1)
    peak_part = jnp.max(valid[:, :, None] * jnp.abs(coef), axis=1)
    energy_all, peak_all = (
        lax.all_to_all(energy_part[None], "rad", split_axis=2, concat_axis=0, tiled=True),
        lax.all_to_all(peak_part[None], "rad", split_axis=2, concat_axis=0, tiled=True),
    )
    energy = jnp.sum(energy_all, axis=0)
    peak = jnp.max(peak_all, axis=0)
    local_sum = jnp.sum(energy, axis=0)
    local_top = jnp.max(peak, axis=0)
    column = lax.psum(local_sum, "ell")
    top = lax.pmax(local_top, "ell")
    column = column + 1e-06
    top = top + 1e-06
    total_ells = ell_ids.shape[0] * lax.axis_size("ell")
    share = total_ells * energy / column[None, :]
    crest = peak / top[None, :]
    return (share, crest)


def solution(mesh):
    in_specs = (P("rad", "ell", None), P("rad", "ell", None), P("ell"))
    out_specs = (P("ell", "rad"), P("ell", "rad"))
    return jax.shard_map(
        per_device, mesh=mesh, in_specs=in_specs, out_specs=out_specs, check_vma=False
    )
```

profile of v0, /device:TPU:0, one launch (start us, length us, event | category | flops | bytes accessed | tf_op | source)
XLA Modules:
  0.0 218.3 jit_solution(14163633866488096663)
XLA Ops:
  7.2 0.0 copy-start
  7.2 0.0 all-gather.2.cloned.1.call-start
  7.2 2.9 %copy.19 = bf16[64,32,256]{2,0,1:T(8,128)(2,1)} copy(bf16[64,32,256]{2,1,0:T(8,128)(2,1)} %param.4) | data formatting | bytes 2097152 | tf_op args[1]
  10.2 0.0 all-gather.2.cloned.1.call-update
  10.2 0.0 copy-done
  10.2 7.8 %copy.17 = bf16[64,32,512]{0,1,2:T(8,128)(2,1)} copy(bf16[64,32,512]{2,1,0:T(8,128)(2,1)S(1)} %copy-done) | data formatting | bytes 4194304 | tf_op args[0]
  18.0 7.7 %reshape.45 = bf16[8,2,65536]{2,1,0:T(2,128)(2,1)} reshape(bf16[512,32,64]{2,1,0:T(8,128)(2,1)} %bitcast.22) | data formatting | bytes 4194304
  25.7 0.0 copy-start.1
  25.7 7.5 %all-to-all-start = ((bf16[8,2,65536]{2,1,0:T(2,128)(2,1)}), bf16[8,2,65536]{2,1,0:T(2,128)(2,1)S(1)}, u32[]{:S(2)}, u32[]{:S(2)}) async-start(bf16[8,2,65536]{2,1,0:T(2,128)(2,1)} %reshape.45), calls=%async_computation | async-start | bytes 4194304 | tf_op jit(solution)/shard_map/all_to_all | solution.py:8
  33.2 0.0 copy-done.1
  33.2 0.1 compare_convert_fusion
  33.2 87.4 %all-to-all-done = bf16[8,2,65536]{2,1,0:T(2,128)(2,1)S(1)} async-done(((bf16[8,2,65536]{2,1,0:T(2,128)(2,1)}), bf16[8,2,65536]{2,1,0:T(2,128)(2,1)S(1)}, u32[]{:S(2)}, u32[]{:S(2)}) %all-to-all-start) | async-done | bytes 2097184 | tf_op jit(solution)/shard_map/all_to_all | solution.py:8
  120.7 5.0 %reshape.46 = bf16[512,32,64]{2,1,0:T(8,128)(2,1)} reshape(bf16[8,2,65536]{2,1,0:T(2,128)(2,1)S(1)} %all-to-all-done) | data formatting | bytes 4194304
  125.7 6.8 %copy.25 = bf16[64,32,8,64]{0,2,3,1:T(8,128)(2,1)} copy(bf16[64,32,8,64]{0,1,3,2:T(8,128)(2,1)} %bitcast.23) | data formatting | bytes 4194304 | tf_op jit(solution)/shard_map/all_to_all | solution.py:8
  132.5 5.4 %all_to_all.34 = bf16[512,32,64]{0,2,1:T(8,128)(2,1)S(1)} reshape(bf16[8,64,32,64]{1,0,3,2:T(8,128)(2,1)} %bitcast.24) | data formatting | bytes 4194304 | tf_op jit(solution)/shard_map/all_to_all | solution.py:8
  137.9 35.0 %all-gather.2.cloned.1.call-done = bf16[512,32,256]{2,0,1:T(8,128)(2,1)} async-done(((bf16[64,32,256]{2,0,1:T(8,128)(2,1)}), bf16[512,32,256]{2,0,1:T(8,128)(2,1)}) %all-gather.2.cloned.1.call-update) | async-done | bytes 8388624 | tf_op jit(solution)/shard_map/all_gather | solution.py:13
  172.9 4.9 %multiply_reduce_fusion = (f32[32,256]{1,0:T(8,128)S(1)}, f32[32,256]{1,0:T(8,128)S(1)}) fusion(f32[32,64]{1,0:T(8,128)S(1)} %compare_convert_fusion, bf16[512,32,64]{0,2,1:T(8,128)(2,1)S(1)} %all_to_all.34, bf16[512,32,256]{2,0,1:T(8,128)(2,1)} %all-gather.2.cloned.1.call-done), kind=kOutput, calls=%fused_computation.3 | convolution fusion | flops 540000256 | bytes 10559488 | tf_op jit(solution)/shard_map/rem,ren->emn/dot_general | solution.py:10
  177.8 0.1 copy.21
  177.9 0.5 broadcast.33
  178.4 1.0 reduce.18
  179.4 0.7 reshape.49
  180.1 3.3 %all-to-all-start.2 = ((f32[8,1,1024]{2,1,0:T(1,128)}), f32[8,1,1024]{2,1,0:T(1,128)S(1)}, u32[]{:S(2)}, u32[]{:S(2)}) async-start(f32[8,1,1024]{2,1,0:T(1,128)} %reshape.49), calls=%async_computation.2 | async-start | bytes 65536 | tf_op jit(solution)/shard_map/all_to_all | solution.py:22
  183.5 0.1 copy.20
  183.6 1.0 reduce.16
  184.6 0.7 reshape.47
  185.3 4.8 %all-to-all-done.2 = f32[8,1,1024]{2,1,0:T(1,128)S(1)} async-done(((f32[8,1,1024]{2,1,0:T(1,128)}), f32[8,1,1024]{2,1,0:T(1,128)S(1)}, u32[]{:S(2)}, u32[]{:S(2)}) %all-to-all-start.2) | async-done | bytes 32800 | tf_op jit(solution)/shard_map/all_to_all | solution.py:22
  190.1 3.3 %all-to-all-start.1 = ((f32[8,1,1024]{2,1,0:T(1,128)}), f32[8,1,1024]{2,1,0:T(1,128)S(1)}, u32[]{:S(2)}, u32[]{:S(2)}) async-start(f32[8,1,1024]{2,1,0:T(1,128)} %reshape.47), calls=%async_computation.1 | async-start | bytes 65536 | tf_op jit(solution)/shard_map/all_to_all | solution.py:21
  193.4 0.7 reduce.19
  194.2 0.2 reshape.50
  194.4 1.0 bitcast_reduce_fusion
  195.4 0.1 reduce_max.37
  195.6 6.0 %pmax.7 = f32[32]{0:T(128)S(1)} all-reduce(f32[32]{0:T(128)S(1)} %reduce_max.38), channel_id=1, replica_groups=mesh['rad'=8,'ell'=4] {'ell'}, use_global_device_ids=true, to_apply=%region_9.10 | all-reduce | flops 32 | bytes 256 | tf_op jit(solution)/shard_map/pmax | solution.py:29
  201.5 0.1 broadcast_divide_fusion
  201.6 0.7 copy.23
  202.3 0.0 all-to-all-done.1
  202.3 0.7 reduce.17
  203.0 0.2 reshape.48
  203.2 1.0 bitcast_reduce_fusion.1
  204.3 0.1 reduce_sum.37
  204.4 6.3 %psum.7 = f32[32]{0:T(128)S(1)} all-reduce(f32[32]{0:T(128)S(1)} %reduce_sum.38), channel_id=1, replica_groups=mesh['rad'=8,'ell'=4] {'ell'}, use_global_device_ids=true, to_apply=%region_4.0 | all-reduce | flops 32 | bytes 256 | tf_op jit(solution)/shard_map/psum | solution.py:28
  210.7 0.1 multiply_divide_fusion
  210.8 0.7 copy.22
  (8 shorter events, 0.1 us)
Async XLA Ops:
  7.2 3.0 %copy-start = (bf16[64,32,512]{2,1,0:T(8,128)(2,1)S(1)}, bf16[64,32,512]{2,1,0:T(8,128)(2,1)}, u32[]{:S(2)}) copy-start(bf16[64,32,512]{2,1,0:T(8,128)(2,1)} %param.3) | copy-start | bytes 6291460
  7.2 165.7 %all-gather.2.cloned.1.call-start = ((), (), s32[]{:S(2)}) async-start(), calls=%async_computation.3 | async-start | bytes 9437184 | tf_op jit(solution)/shard_map/all_gather | solution.py:13
  25.7 7.5 %copy-start.1 = (s32[32]{0:T(128)S(1)}, s32[32]{0:T(128)}, u32[]{:S(2)}) copy-start(s32[32]{0:T(128)} %param.5) | copy-start | bytes 388
  25.7 95.0 %all-to-all-start = ((bf16[8,2,65536]{2,1,0:T(2,128)(2,1)}), bf16[8,2,65536]{2,1,0:T(2,128)(2,1)S(1)}, u32[]{:S(2)}, u32[]{:S(2)}) async-start(bf16[8,2,65536]{2,1,0:T(2,128)(2,1)} %reshape.45), calls=%async_computation | async-start | bytes 4194304 | tf_op jit(solution)/shard_map/all_to_all | solution.py:8
  180.1 10.0 %all-to-all-start.2 = ((f32[8,1,1024]{2,1,0:T(1,128)}), f32[8,1,1024]{2,1,0:T(1,128)S(1)}, u32[]{:S(2)}, u32[]{:S(2)}) async-start(f32[8,1,1024]{2,1,0:T(1,128)} %reshape.49), calls=%async_computation.2 | async-start | bytes 65536 | tf_op jit(solution)/shard_map/all_to_all | solution.py:22
  190.1 12.2 %all-to-all-start.1 = ((f32[8,1,1024]{2,1,0:T(1,128)}), f32[8,1,1024]{2,1,0:T(1,128)S(1)}, u32[]{:S(2)}, u32[]{:S(2)}) async-start(f32[8,1,1024]{2,1,0:T(1,128)} %reshape.47), calls=%async_computation.1 | async-start | bytes 65536 | tf_op jit(solution)/shard_map/all_to_all | solution.py:21
Sparse Core Ops, SparseCore 0:
  10.3 162.5 all-gather.1
where the time goes:
time: 219 us; the launch traced here: 218 us
  waiting for transfers between devices  127 us (58%)
  local copies, waits for them, and re-layouts  39.8 us (18%)
  starting transfers between devices  14.2 us (6%)
  between operations  14.2 us (6%)
  blocking collectives  12.3 us (6%)
  other arithmetic  5.77 us (3%)
  matrix products  4.92 us (2%)
    all_to_all x1, waiting for transfers between devices, per_device(): lax.all_to_all(field, 'rad', split_axis=2, concat_axis=0, tiled=True)  87.4 us
    all_gather x1, waiting for transfers between devices, per_device(): lax.all_gather(projection, 'rad', axis=0, tiled=True)  35 us
    unnamed x15, local copies, waits for them, and re-layouts  27.2 us
    all_to_all x2, local copies, waits for them, and re-layouts, per_device(): lax.all_to_all(field, 'rad', split_axis=2, concat_axis=0, tiled=True)  12.2 us
    all_to_all x1, starting transfers between devices, per_device(): lax.all_to_all(field, 'rad', split_axis=2, concat_axis=0, tiled=True)  7.47 us
    psum x1, blocking collectives, per_device(): column = lax.psum(local_sum, 'ell')  6.3 us
    pmax x1, blocking collectives, per_device(): top = lax.pmax(local_top, 'ell')  5.96 us
    dot_general x1, matrix products, per_device(): jnp.einsum('rem,ren->emn', exchanged, lax.all_gather(projection, 'rad', a...  4.92 us
  transfers between devices with their start and end apart: 4, of which 3 were waited for; matrix products, arithmetic and copies ran while one was open for 15% of the time, Pallas kernels for 0%

commit v1 on v0

--- a/solution.py
+++ b/solution.py
@@ -7,12 +7,38 @@
 def per_device(field, projection, ell_ids):
     exchanged = lax.all_to_all(field, "rad", split_axis=2, concat_axis=0, tiled=True)
     slot_share = exchanged.shape[2]
-    coef = jnp.einsum(
+    devices, index, width = (lax.axis_size("rad"), lax.axis_index("rad"), projection.shape[0])
+    ahead = [(i, (i + 1) % devices) for i in range(devices)]
+    left = [(i, (i - 1) % devices) for i in range(devices)]
+    half = devices // 2
+    from_left = from_right = projection
+    so_far = jnp.einsum(
         "rem,ren->emn",
-        exchanged,
-        lax.all_gather(projection, "rad", axis=0, tiled=True),
+        lax.dynamic_slice_in_dim(exchanged, index * width, projection.shape[0], axis=0),
+        projection,
         preferred_element_type=jnp.float32,
     )
+    for step in range(1, half + 1):
+        from_left = lax.ppermute(from_left, "rad", ahead)
+        if step < devices - half:
+            from_right = lax.ppermute(from_right, "rad", left)
+            so_far = so_far + jnp.einsum(
+                "rem,ren->emn",
+                lax.dynamic_slice_in_dim(
+                    exchanged, (index + step) % devices * width, from_right.shape[0], axis=0
+                ),
+                from_right,
+                preferred_element_type=jnp.float32,
+            )
+        so_far = so_far + jnp.einsum(
+            "rem,ren->emn",
+            lax.dynamic_slice_in_dim(
+                exchanged, (index - step) % devices * width, from_left.shape[0], axis=0
+            ),
+            from_left,
+            preferred_element_type=jnp.float32,
+        )
+    coef = so_far
     slots = lax.axis_index("rad") * slot_share + jnp.arange(slot_share, dtype=jnp.int32)
     valid = (slots[None, :] < 2 * ell_ids[:, None] + 1).astype(jnp.float32)
     energy_part = jnp.sum(valid[:, :, None] * coef * coef, axis=1)

time: 219 us -> 255 us (1.16)
  starting transfers between devices: 14.2 us -> 37.3 us
  waiting for transfers between devices: 127 us -> 147 us
  between operations: 14.2 us -> 0.83 us
  matrix products: 4.92 us -> 13 us
    ppermute x0 -> x7, waiting for transfers between devices: none -> 142 us  [the longest x4 142 us: per_device(): from_left = lax.ppermute(from_left, 'rad', ahead)]
    all_to_all x1, waiting for transfers between devices: 87.4 us -> 0.01 us  [per_device(): lax.all_to_all(field, 'rad', split_axis=2, concat_axis=0, tiled=True)]
    all_gather x1 -> x0, waiting for transfers between devices: 35 us -> none  [per_device(): lax.all_gather(projection, 'rad', axis=0, tiled=True)]
    ppermute x0 -> x7, starting transfers between devices: none -> 19.9 us  [the longest x3 10.2 us: per_device(): from_right = lax.ppermute(from_right, 'rad', left)]
    dot_general x1 -> x8, matrix products: 4.92 us -> 13 us  [the longest x4 6.84 us: per_device(): jnp.einsum('rem,ren->emn', lax.dynamic_slice_in_dim(exchanged, (index - s...]
    all_to_all x1, waiting for transfers between devices: 0.01 us -> 4.89 us  [per_device(): lax.all_to_all(energy_part[None], 'rad', split_axis=2, concat_axis=0, til...]
    all_to_all x1, waiting for transfers between devices: 4.82 us -> 0.01 us  [per_device(): lax.all_to_all(peak_part[None], 'rad', split_axis=2, concat_axis=0, tiled...]
    all_to_all x1, starting transfers between devices: 3.33 us -> 6.65 us  [per_device(): lax.all_to_all(energy_part[None], 'rad', split_axis=2, concat_axis=0, til...]
  transfers between devices with their start and end apart: 4 -> 10, of which waited for: 3 -> 4; matrix products, arithmetic and copies ran while one was open for 15% -> 11% of each run, Pallas kernels for 0% -> 0%
where the time goes in v1:
time: 255 us; the launch traced here: 254 us
  waiting for transfers between devices  147 us (58%)
  local copies, waits for them, and re-layouts  38.3 us (15%)
  starting transfers between devices  37.3 us (15%)
  matrix products  13 us (5%)
  blocking collectives  12.3 us (5%)
  other arithmetic  5.77 us (2%)
    ppermute x4, waiting for transfers between devices, per_device(): from_left = lax.ppermute(from_left, 'rad', ahead)  142 us
    unnamed x19, local copies, waits for them, and re-layouts  25.7 us
    all_to_all x2, local copies, waits for them, and re-layouts, per_device(): lax.all_to_all(field, 'rad', split_axis=2, concat_axis=0, tiled=True)  12.2 us
    ppermute x3, starting transfers between devices, per_device(): from_right = lax.ppermute(from_right, 'rad', left)  10.2 us
    ppermute x4, starting transfers between devices, per_device(): from_left = lax.ppermute(from_left, 'rad', ahead)  9.61 us
    all_to_all x1, starting transfers between devices, per_device(): lax.all_to_all(field, 'rad', split_axis=2, concat_axis=0, tiled=True)  7.44 us
    dot_general x4, matrix products, per_device(): jnp.einsum('rem,ren->emn', lax.dynamic_slice_in_dim(exchanged, (index - s...  6.84 us
    all_to_all x1, starting transfers between devices, per_device(): lax.all_to_all(energy_part[None], 'rad', split_axis=2, concat_axis=0, til...  6.65 us
  transfers between devices with their start and end apart: 10, of which 4 were waited for; matrix products, arithmetic and copies ran while one was open for 11% of the time, Pallas kernels for 0%

profile of v1, /device:TPU:0, one launch (start us, length us, event | category | flops | bytes accessed | tf_op | source)
XLA Modules:
  0.0 254.5 jit_solution(3146356647617033237)
XLA Ops:
  0.6 8.8 %copy.23 = bf16[64,32,512]{0,1,2:T(8,128)(2,1)} copy(bf16[64,32,512]{2,1,0:T(8,128)(2,1)} %param.3) | data formatting | bytes 4194304 | tf_op args[0]
  9.4 7.6 %reshape.45 = bf16[8,2,65536]{2,1,0:T(2,128)(2,1)} reshape(bf16[512,32,64]{2,1,0:T(8,128)(2,1)} %bitcast.27) | data formatting | bytes 4194304
  17.0 0.0 copy-start
  17.0 7.4 %all-to-all-start = ((bf16[8,2,65536]{2,1,0:T(2,128)(2,1)}), bf16[8,2,65536]{2,1,0:T(2,128)(2,1)S(1)}, u32[]{:S(2)}, u32[]{:S(2)}) async-start(bf16[8,2,65536]{2,1,0:T(2,128)(2,1)} %reshape.45), calls=%async_computation | async-start | bytes 4194304 | tf_op jit(solution)/shard_map/all_to_all | solution.py:8
  24.4 0.0 copy-done
  24.4 0.0 copy-start.3
  24.4 0.6 copy.25
  25.0 2.1 collective-permute-start.1
  27.1 2.8 %collective-permute-start = (bf16[64,32,256]{2,0,1:T(8,128)(2,1)S(1)}, bf16[64,32,256]{2,0,1:T(8,128)(2,1)}, u32[]{:S(2)}, u32[]{:S(2)}) collective-permute-start(bf16[64,32,256]{2,0,1:T(8,128)(2,1)S(1)} %copy.25), channel_id=1, source_target_pairs={{0,28},{4,0},{8,4},{12,8},{16,12},{20,16},{24,20},{28,24},{1,29},{... | collective-permute-start | bytes 3145736 | tf_op jit(solution)/shard_map/ppermute | solution.py:24
  29.8 62.1 %collective-permute-done.1 = bf16[64,32,256]{2,0,1:T(8,128)(2,1)S(1)} collective-permute-done((bf16[64,32,256]{2,0,1:T(8,128)(2,1)S(1)}, bf16[64,32,256]{2,0,1:T(8,128)(2,1)S(1)}, u32[]{:S(2)}, u32[]{:S(2)}) %collective-permute-start.1) | collective-permute-done | bytes 1048608 | tf_op jit(solution)/shard_map/ppermute | solution.py:22
  92.0 0.0 copy-start.1
  92.0 2.5 collective-permute-start.3
  94.5 0.0 collective-permute-done
  94.5 0.0 copy-done.1
  94.5 3.7 %collective-permute-start.2 = (bf16[64,32,256]{2,0,1:T(8,128)(2,1)}, bf16[64,32,256]{2,0,1:T(8,128)(2,1)}, u32[]{:S(2)}, u32[]{:S(2)}) collective-permute-start(bf16[64,32,256]{2,0,1:T(8,128)(2,1)} %collective-permute-done), channel_id=1, source_target_pairs={{0,28},{4,0},{8,4},{12,8},{16,12},{20,16},{24,20},{28,24},{1,29},{... | collective-permute-start | bytes 3145736 | tf_op jit(solution)/shard_map/ppermute | solution.py:24
  98.2 40.3 %collective-permute-done.3 = bf16[64,32,256]{2,0,1:T(8,128)(2,1)} collective-permute-done((bf16[64,32,256]{2,0,1:T(8,128)(2,1)S(1)}, bf16[64,32,256]{2,0,1:T(8,128)(2,1)}, u32[]{:S(2)}, u32[]{:S(2)}) %collective-permute-start.3) | collective-permute-done | bytes 1048608 | tf_op jit(solution)/shard_map/ppermute | solution.py:22
  138.5 2.6 %collective-permute-start.5 = (bf16[64,32,256]{2,0,1:T(8,128)(2,1)}, bf16[64,32,256]{2,0,1:T(8,128)(2,1)}, u32[]{:S(2)}, u32[]{:S(2)}) collective-permute-start(bf16[64,32,256]{2,0,1:T(8,128)(2,1)} %collective-permute-done.3), channel_id=1, source_target_pairs={{0,4},{4,8},{8,12},{12,16},{16,20},{20,24},{24,28},{28,0},{1,5},{5... | collective-permute-start | bytes 3145736 | tf_op jit(solution)/shard_map/ppermute | solution.py:22
  141.1 0.0 copy-done.3
  141.1 0.1 compare_convert_fusion
  141.2 0.0 collective-permute-done.2
  141.2 3.7 %collective-permute-start.4 = (bf16[64,32,256]{2,0,1:T(8,128)(2,1)}, bf16[64,32,256]{2,0,1:T(8,128)(2,1)}, u32[]{:S(2)}, u32[]{:S(2)}) collective-permute-start(bf16[64,32,256]{2,0,1:T(8,128)(2,1)} %collective-permute-done.2), channel_id=1, source_target_pairs={{0,28},{4,0},{8,4},{12,8},{16,12},{20,16},{24,20},{28,24},{1,29},{... | collective-permute-start | bytes 3145736 | tf_op jit(solution)/shard_map/ppermute | solution.py:24
  144.9 39.7 %collective-permute-done.5 = bf16[64,32,256]{2,0,1:T(8,128)(2,1)} collective-permute-done((bf16[64,32,256]{2,0,1:T(8,128)(2,1)}, bf16[64,32,256]{2,0,1:T(8,128)(2,1)}, u32[]{:S(2)}, u32[]{:S(2)}) %collective-permute-start.5) | collective-permute-done | bytes 1048608 | tf_op jit(solution)/shard_map/ppermute | solution.py:22
  184.6 2.5 collective-permute-start.6
  187.1 0.0 all-to-all-done
  187.1 5.0 %reshape.46 = bf16[512,32,64]{2,1,0:T(8,128)(2,1)} reshape(bf16[8,2,65536]{2,1,0:T(2,128)(2,1)S(1)} %all-to-all-done) | data formatting | bytes 4194304
  192.1 6.9 %copy.35 = bf16[64,32,8,64]{0,2,3,1:T(8,128)(2,1)} copy(bf16[64,32,8,64]{0,1,3,2:T(8,128)(2,1)} %bitcast.28) | data formatting | bytes 4194304 | tf_op jit(solution)/shard_map/all_to_all | solution.py:8
  198.9 5.4 %all_to_all.34 = bf16[512,32,64]{0,2,1:T(8,128)(2,1)S(1)} reshape(bf16[8,64,32,64]{1,0,3,2:T(8,128)(2,1)} %bitcast.29) | data formatting | bytes 4194304 | tf_op jit(solution)/shard_map/all_to_all | solution.py:8
  204.3 1.0 fusion.14
  205.3 1.7 fusion.2
  207.0 1.7 fusion.6
  208.7 0.0 copy-start.2
  208.7 1.8 fusion.8
  210.5 0.0 copy-done.2
  210.5 0.5 fusion.10
  211.0 1.7 fusion.12
  212.8 0.0 collective-permute-done.4
  212.8 1.7 fusion.4
  214.5 0.0 collective-permute-done.6
  214.5 2.9 %multiply_reduce_fusion = (f32[32,256]{1,0:T(8,128)S(1)}, f32[32,256]{1,0:T(8,128)S(1)}) fusion(f32[32,64]{1,0:T(8,128)S(1)} %compare_convert_fusion, bf16[64,32,256]{2,0,1:T(8,128)(2,1)} %collective-permute-done.6, bf16[512,32,64]{0,2,1:T(8,128)(2,1)S(1)} %all_to_all.34, s32[]{:T(128)S(6)} %select_n.69, f32[32,64,256]{2,1,0:T(8,128)S(1)} %fusion.2, ...), kind=kOutput, calls=%fused_computation.3 | convolution fusion | flops 73908224 | bytes 16334852 | tf_op jit(solution)/shard_map/rem,ren->emn/dot_general | solution.py:33
  217.4 0.1 copy.28
  217.5 0.5 broadcast.40
  218.1 1.0 reduce.16
  219.0 0.7 reshape.47
  219.7 6.6 %all-to-all-start.1 = ((f32[8,1,1024]{2,1,0:T(1,128)}), f32[8,1,1024]{2,1,0:T(1,128)S(1)}, u32[]{:S(2)}, u32[]{:S(2)}) async-start(f32[8,1,1024]{2,1,0:T(1,128)} %reshape.47), calls=%async_computation.1 | async-start | bytes 65536 | tf_op jit(solution)/shard_map/all_to_all | solution.py:47
  226.4 0.1 copy.29
  226.5 1.0 reduce.18
  227.5 0.7 reshape.49
  228.2 4.9 %all-to-all-done.1 = f32[8,1,1024]{2,1,0:T(1,128)S(1)} async-done(((f32[8,1,1024]{2,1,0:T(1,128)}), f32[8,1,1024]{2,1,0:T(1,128)S(1)}, u32[]{:S(2)}, u32[]{:S(2)}) %all-to-all-start.1) | async-done | bytes 32800 | tf_op jit(solution)/shard_map/all_to_all | solution.py:47
  233.1 3.3 %all-to-all-start.2 = ((f32[8,1,1024]{2,1,0:T(1,128)}), f32[8,1,1024]{2,1,0:T(1,128)S(1)}, u32[]{:S(2)}, u32[]{:S(2)}) async-start(f32[8,1,1024]{2,1,0:T(1,128)} %reshape.49), calls=%async_computation.2 | async-start | bytes 65536 | tf_op jit(solution)/shard_map/all_to_all | solution.py:48
  236.4 0.7 reduce.17
  237.1 0.2 reshape.48
  237.4 1.0 bitcast_reduce_fusion.1
  238.4 0.1 reduce_sum.37
  238.5 6.0 %psum.7 = f32[32]{0:T(128)S(1)} all-reduce(f32[32]{0:T(128)S(1)} %reduce_sum.38), channel_id=1, replica_groups=mesh['rad'=8,'ell'=4] {'ell'}, use_global_device_ids=true, to_apply=%region_4.5 | all-reduce | flops 32 | bytes 256 | tf_op jit(solution)/shard_map/psum | solution.py:54
  244.5 0.1 multiply_divide_fusion
  244.6 0.7 copy.30
  245.3 0.0 all-to-all-done.2
  245.3 0.7 reduce.19
  246.0 0.2 reshape.50
  246.2 1.0 bitcast_reduce_fusion
  247.2 0.1 reduce_max.37
  247.4 6.3 %pmax.7 = f32[32]{0:T(128)S(1)} all-reduce(f32[32]{0:T(128)S(1)} %reduce_max.38), channel_id=1, replica_groups=mesh['rad'=8,'ell'=4] {'ell'}, use_global_device_ids=true, to_apply=%region_9.10 | all-reduce | flops 32 | bytes 256 | tf_op jit(solution)/shard_map/pmax | solution.py:55
  253.7 0.1 broadcast_divide_fusion
  253.8 0.7 copy.31
  (8 shorter events, 0.1 us)
Async XLA Ops:
  17.0 7.4 %copy-start = (bf16[64,32,256]{2,1,0:T(8,128)(2,1)S(1)}, bf16[64,32,256]{2,1,0:T(8,128)(2,1)}, u32[]{:S(2)}) copy-start(bf16[64,32,256]{2,1,0:T(8,128)(2,1)} %param.4) | copy-start | bytes 3145732
  17.0 170.1 %all-to-all-start = ((bf16[8,2,65536]{2,1,0:T(2,128)(2,1)}), bf16[8,2,65536]{2,1,0:T(2,128)(2,1)S(1)}, u32[]{:S(2)}, u32[]{:S(2)}) async-start(bf16[8,2,65536]{2,1,0:T(2,128)(2,1)} %reshape.45), calls=%async_computation | async-start | bytes 4194304 | tf_op jit(solution)/shard_map/all_to_all | solution.py:8
  24.4 116.7 %copy-start.3 = (s32[32]{0:T(128)S(1)}, s32[32]{0:T(128)}, u32[]{:S(2)}) copy-start(s32[32]{0:T(128)} %param.5) | copy-start | bytes 388
  25.0 67.0 %collective-permute-start.1 = (bf16[64,32,256]{2,0,1:T(8,128)(2,1)S(1)}, bf16[64,32,256]{2,0,1:T(8,128)(2,1)S(1)}, u32[]{:S(2)}, u32[]{:S(2)}) collective-permute-start(bf16[64,32,256]{2,0,1:T(8,128)(2,1)S(1)} %copy.25), channel_id=1, source_target_pairs={{0,4},{4,8},{8,12},{12,16},{16,20},{20,24},{24,28},{28,0},{1,5},{5... | collective-permute-start | bytes 3145736 | tf_op jit(solution)/shard_map/ppermute | solution.py:22
  27.1 67.4 %collective-permute-start = (bf16[64,32,256]{2,0,1:T(8,128)(2,1)S(1)}, bf16[64,32,256]{2,0,1:T(8,128)(2,1)}, u32[]{:S(2)}, u32[]{:S(2)}) collective-permute-start(bf16[64,32,256]{2,0,1:T(8,128)(2,1)S(1)} %copy.25), channel_id=1, source_target_pairs={{0,28},{4,0},{8,4},{12,8},{16,12},{20,16},{24,20},{28,24},{1,29},{... | collective-permute-start | bytes 3145736 | tf_op jit(solution)/shard_map/ppermute | solution.py:24
  92.0 2.5 copy-start.1
  92.0 46.5 %collective-permute-start.3 = (bf16[64,32,256]{2,0,1:T(8,128)(2,1)S(1)}, bf16[64,32,256]{2,0,1:T(8,128)(2,1)}, u32[]{:S(2)}, u32[]{:S(2)}) collective-permute-start(bf16[64,32,256]{2,0,1:T(8,128)(2,1)S(1)} %collective-permute-done.1), channel_id=1, source_target_pairs={{0,4},{4,8},{8,12},{12,16},{16,20},{20,24},{24,28},{28,0},{1,5},{5... | collective-permute-start | bytes 3145736 | tf_op jit(solution)/shard_map/ppermute | solution.py:22
  94.5 46.7 %collective-permute-start.2 = (bf16[64,32,256]{2,0,1:T(8,128)(2,1)}, bf16[64,32,256]{2,0,1:T(8,128)(2,1)}, u32[]{:S(2)}, u32[]{:S(2)}) collective-permute-start(bf16[64,32,256]{2,0,1:T(8,128)(2,1)} %collective-permute-done), channel_id=1, source_target_pairs={{0,28},{4,0},{8,4},{12,8},{16,12},{20,16},{24,20},{28,24},{1,29},{... | collective-permute-start | bytes 3145736 | tf_op jit(solution)/shard_map/ppermute | solution.py:24
  138.5 46.1 %collective-permute-start.5 = (bf16[64,32,256]{2,0,1:T(8,128)(2,1)}, bf16[64,32,256]{2,0,1:T(8,128)(2,1)}, u32[]{:S(2)}, u32[]{:S(2)}) collective-permute-start(bf16[64,32,256]{2,0,1:T(8,128)(2,1)} %collective-permute-done.3), channel_id=1, source_target_pairs={{0,4},{4,8},{8,12},{12,16},{16,20},{20,24},{24,28},{28,0},{1,5},{5... | collective-permute-start | bytes 3145736 | tf_op jit(solution)/shard_map/ppermute | solution.py:22
  141.2 71.6 %collective-permute-start.4 = (bf16[64,32,256]{2,0,1:T(8,128)(2,1)}, bf16[64,32,256]{2,0,1:T(8,128)(2,1)}, u32[]{:S(2)}, u32[]{:S(2)}) collective-permute-start(bf16[64,32,256]{2,0,1:T(8,128)(2,1)} %collective-permute-done.2), channel_id=1, source_target_pairs={{0,28},{4,0},{8,4},{12,8},{16,12},{20,16},{24,20},{28,24},{1,29},{... | collective-permute-start | bytes 3145736 | tf_op jit(solution)/shard_map/ppermute | solution.py:24
  184.6 29.9 %collective-permute-start.6 = (bf16[64,32,256]{2,0,1:T(8,128)(2,1)}, bf16[64,32,256]{2,0,1:T(8,128)(2,1)}, u32[]{:S(2)}, u32[]{:S(2)}) collective-permute-start(bf16[64,32,256]{2,0,1:T(8,128)(2,1)} %collective-permute-done.5), channel_id=1, source_target_pairs={{0,4},{4,8},{8,12},{12,16},{16,20},{20,24},{24,28},{28,0},{1,5},{5... | collective-permute-start | bytes 3145736 | tf_op jit(solution)/shard_map/ppermute | solution.py:22
  208.7 1.8 copy-start.2
  219.7 13.3 %all-to-all-start.1 = ((f32[8,1,1024]{2,1,0:T(1,128)}), f32[8,1,1024]{2,1,0:T(1,128)S(1)}, u32[]{:S(2)}, u32[]{:S(2)}) async-start(f32[8,1,1024]{2,1,0:T(1,128)} %reshape.47), calls=%async_computation.1 | async-start | bytes 65536 | tf_op jit(solution)/shard_map/all_to_all | solution.py:47
  233.1 12.2 %all-to-all-start.2 = ((f32[8,1,1024]{2,1,0:T(1,128)}), f32[8,1,1024]{2,1,0:T(1,128)S(1)}, u32[]{:S(2)}, u32[]{:S(2)}) async-start(f32[8,1,1024]{2,1,0:T(1,128)} %reshape.49), calls=%async_computation.2 | async-start | bytes 65536 | tf_op jit(solution)/shard_map/all_to_all | solution.py:48
